TPU v7x, 128 devices: a whole 4x4x4 slice. The times are simulated.
128 devices in a mesh: row: 8 (over z_hi, y), col: 16 (over x, z_lo, core).
Axes of the slice: x: 4, y: 4, z: 4 (z_hi: 2, z_lo: 2; z = z_hi * 2 + z_lo), core: 2. Of those that a mesh axis runs over, the one named last changes fastest.
Arguments:
- features: bfloat16 [16, 8192, 128], P('col', 'row'), may hold values from 0.099609375 to 3
- relu_mask: int32 [16, 8192, 128], P('col', 'row'), may hold values 0 or 1
- tiles: bfloat16 [8, 16, 184, 256, 256], P('row', 'col'), may hold values from -0.25 to 0.25
- tile_rows: int32 [8, 16, 184], P('row', 'col'), may hold values from 0 to 63, as said below
- tile_cols: int32 [8, 16, 184], P('row', 'col'), may hold values from 0 to 31
- tile_count: int32 [8, 16], P('row', 'col'), may hold values from 23 to 184, as said below
- weight: bfloat16 [128, 128], replicated, may hold values from -0.5 to 0.5
- cotangent: bfloat16 [8, 16384, 128], P('row', 'col'), may hold values from -6 to 6
Outputs:
- out_pre: bfloat16 [8, 16384, 128], P('row', 'col')
- weight_grad: float32 [128, 128], replicated
- input_grad: bfloat16 [16, 8192, 128], P('col', 'row')
Inputs may be any that keep to these rules, and one draw needn't show every extreme that they name: `tile_rows`: within one panel pair the live and dead slots name distinct (block row, block column) pairs. `tile_count`: counts differ widely between panel pairs.
All inputs are finite; a program needn't handle non-finite values. No bound on the sum of `relu_mask` on one device may be relied on, other than what follows from the above.
Results may differ from a plain program's by a relative error of at most 0.022.
Values may be sent and summed in bfloat16 or wider, within the bound.
A program may use at most 192 MiB of HBM per device.

v0:
```python
import jax
import jax.numpy as jnp
from jax import lax
from jax.sharding import PartitionSpec as P


def slot_products(tile_vals, row_ids, col_ids, source, backward):
    tile_size = tile_vals.shape[1]
    feature_width = source.shape[1]
    if backward:
        blocks = source.reshape(-1, tile_size, feature_width)[row_ids]
        products = jnp.einsum("sij,sif->sjf", tile_vals, blocks, preferred_element_type=jnp.float32)
        target_ids = col_ids
    else:
        blocks = source.reshape(-1, tile_size, feature_width)[col_ids]
        products = jnp.einsum("sij,sjf->sif", tile_vals, blocks, preferred_element_type=jnp.float32)
        target_ids = row_ids
    return (products, target_ids)


def apply_tiles(tile_vals, row_ids, col_ids, live_count, source, backward, segments):
    feature_width = source.shape[1]
    slots = tile_vals.shape[0]
    products, target_ids = slot_products(tile_vals, row_ids, col_ids, source, backward)
    live_slots = jnp.arange(slots, dtype=jnp.int32) < live_count
    targets = jnp.arange(segments, dtype=jnp.int32)[:, None] == target_ids[None, :]
    selector = jnp.where(targets & live_slots[None, :], 1.0, 0.0).astype(jnp.float32)
    total = jnp.einsum(
        "rs,sif->rif",
        selector,
        products,
        precision=lax.Precision.HIGHEST,
        preferred_element_type=jnp.float32,
    )
    return total.reshape(-1, feature_width)


def body(features, relu_mask, tiles, tile_rows, tile_cols, tile_count, weight, cotangent):
    tile_size = tiles.shape[3]
    mask_rows = relu_mask[0]
    hidden = features[0] * mask_rows.astype(jnp.bfloat16)
    tile_vals = tiles[0, 0]
    row_ids = tile_rows[0, 0]
    col_ids = tile_cols[0, 0]
    live_count = tile_count[0, 0]
    own_rows = hidden.shape[0]
    row_blocks = own_rows * lax.axis_size("col") // tile_size
    col_blocks = own_rows * lax.axis_size("row") // tile_size
    feat_panel = lax.all_gather(hidden, "row", axis=0, tiled=True)
    forward_terms = apply_tiles(
        tile_vals, row_ids, col_ids, live_count, feat_panel, False, row_blocks
    )
    forward_terms = lax.optimization_barrier(forward_terms.astype(jnp.bfloat16)).astype(jnp.float32)
    aggregate = lax.psum_scatter(
        forward_terms.astype(jnp.bfloat16), "col", scatter_dimension=0, tiled=True
    )
    out_pre = jnp.dot(aggregate, weight, preferred_element_type=jnp.float32).astype(jnp.bfloat16)
    cot_rows = cotangent[0]
    weight_term = lax.dot_general(
        aggregate, cot_rows, (((0,), (0,)), ((), ())), preferred_element_type=jnp.float32
    )
    grad_scale = 1.0 / jnp.sqrt(jnp.float32(own_rows * lax.axis_size("row") * lax.axis_size("col")))
    weight_grad = lax.psum(weight_term, ("row", "col")) * grad_scale
    grad_rows = lax.dot_general(
        cot_rows, weight, (((1,), (1,)), ((), ())), preferred_element_type=jnp.float32
    )
    grad_rows = lax.all_gather(grad_rows.astype(jnp.bfloat16), "col", axis=0, tiled=True)
    back_terms = apply_tiles(tile_vals, row_ids, col_ids, live_count, grad_rows, True, col_blocks)
    back_terms = lax.optimization_barrier(back_terms.astype(jnp.bfloat16)).astype(jnp.float32)
    summed = lax.psum_scatter(
        back_terms.astype(jnp.bfloat16), "row", scatter_dimension=0, tiled=True
    ).astype(jnp.float32)
    input_grad = (summed * mask_rows.astype(jnp.float32)).astype(jnp.bfloat16)
    return (out_pre[None], weight_grad, input_grad[None])


def solution(mesh):
    placed = (
        P("col", "row", None),
        P("col", "row", None),
        P("row", "col", None, None, None),
        P("row", "col", None),
        P("row", "col", None),
        P("row", "col"),
        P(),
        P("row", "col", None),
    )
    return jax.shard_map(
        body,
        mesh=mesh,
        in_specs=placed,
        out_specs=(P("row", "col", None), P(), P("col", "row", None)),
        check_vma=False,
    )
```

profile of v0, /device:TPU:1, one launch (start us, length us, event | category | flops | bytes accessed | tf_op | source)
XLA Modules:
  0.0 451.2 jit_solution(6644754055595961643)
XLA Ops:
  7.2 0.0 copy-start
  7.2 0.0 all-gather.6.cloned.1.call-start
  7.2 1.9 convert_multiply_fusion
  9.1 0.0 all-gather.6.cloned.1.call-update
  9.1 0.0 all-gather.4.cloned.1.call-start
  9.2 0.0 copy-done
  9.2 1.7 convolution_convert_fusion
  10.9 0.0 all-gather.4.cloned.1.call-update
  10.9 0.0 reduce-scatter.3.cloned.1.call-start
  11.6 0.7 compare_select_fusion.1
  12.3 55.5 %all-gather.6.cloned.1.call-done = bf16[1,8192,128]{2,1,0:T(8,128)(2,1)} async-done(((bf16[1,1024,128]{2,1,0:T(8,128)(2,1)}), bf16[1,8192,128]{2,1,0:T(8,128)(2,1)}) %all-gather.6.cloned.1.call-update) | async-done | bytes 2097168 | tf_op jit(solution)/shard_map/all_gather | solution.py:49
  67.9 9.7 %gather_fusion = bf16[184,256,128]{2,1,0:T(8,128)(2,1)} fusion(bf16[32,256,128]{2,1,0:T(8,128)(2,1)} %bitcast.56, s32[1024]{0:T(1024)S(1)} %pad_clamp_fusion.1), kind=kCustom, calls=%fused_computation | custom fusion | bytes 24117984 | tf_op jit(solution)/shard_map/gather | solution.py:15
  77.5 21.6 %fusion.6 = f32[184,128,256]{2,1,0:T(8,128)} fusion(bf16[184,256,128]{2,1,0:T(8,128)(2,1)} %gather_fusion, bf16[1,1,184,256,256]{4,3,2,1,0:T(8,128)(2,1)} %param.10), kind=kOutput, calls=%fused_computation.8 | convolution fusion | flops 3087007744 | bytes 60293120 | tf_op jit(solution)/shard_map/sij,sjf->sif/dot_general | solution.py:16
  99.1 0.0 copy-start.3
  99.1 24.6 %copy.13 = f32[184,128,256]{1,0,2:T(8,128)} copy(f32[184,128,256]{2,1,0:T(8,128)} %fusion.6) | data formatting | bytes 48234496 | tf_op jit(solution)/shard_map/sij,sjf->sif/dot_general | solution.py:16
  123.7 0.0 copy-done.3
  123.7 20.8 %fusion.8 = bf16[64,256,128]{2,0,1:T(8,128)(2,1)S(1)} fusion(f32[184,128,256]{1,0,2:T(8,128)} %copy.13, s32[184]{0:T(256)S(1)} %bitcast.60, pred[184]{0:T(512)(128)(4,1)S(1)} %iota_compare_fusion.2), kind=kOutput, calls=%fused_computation.10 | convolution fusion | flops 4632644096 | bytes 28312472 | tf_op jit(solution)/shard_map/rs,sif->rif/dot_general | solution.py:28
  144.5 4.7 %copy.11 = bf16[64,256,128]{2,1,0:T(8,128)(2,1)} copy(bf16[64,256,128]{2,0,1:T(8,128)(2,1)S(1)} %fusion.8) | data formatting | bytes 8388608 | tf_op jit(solution)/shard_map/convert_element_type | solution.py:53
  149.1 0.0 reduce-scatter.3.cloned.1.call-update
  149.2 0.0 reduce-scatter.5.cloned.1.call-start
  149.2 0.0 all-gather.4.cloned.1.call-done
  149.3 10.3 %gather_fusion.1 = bf16[184,256,128]{2,1,0:T(8,128)(2,1)} fusion(bf16[64,256,128]{2,1,0:T(8,128)(2,1)} %bitcast.57, s32[1024]{0:T(1024)S(1)} %pad_clamp_fusion), kind=kCustom, calls=%fused_computation.1 | custom fusion | bytes 24117984 | tf_op jit(solution)/shard_map/gather | solution.py:11
  159.5 22.0 %fusion.4 = f32[184,128,256]{2,1,0:T(8,128)} fusion(bf16[184,256,128]{2,1,0:T(8,128)(2,1)} %gather_fusion.1, bf16[1,1,184,256,256]{4,3,2,1,0:T(8,128)(2,1)} %param.10), kind=kOutput, calls=%fused_computation.6 | convolution fusion | flops 3087007744 | bytes 60293120 | tf_op jit(solution)/shard_map/sij,sif->sjf/dot_general | solution.py:12
  181.6 0.0 copy-start.4
  181.6 24.6 %copy.14 = f32[184,128,256]{1,0,2:T(8,128)} copy(f32[184,128,256]{2,1,0:T(8,128)} %fusion.4) | data formatting | bytes 48234496 | tf_op jit(solution)/shard_map/sij,sif->sjf/dot_general | solution.py:12
  206.2 0.0 copy-done.4
  206.2 0.0 copy-start.2
  206.2 0.0 copy-start.1
  206.2 17.1 %fusion.11 = bf16[32,256,128]{2,0,1:T(8,128)(2,1)S(1)} fusion(f32[184,128,256]{1,0,2:T(8,128)} %copy.14, s32[184]{0:T(256)S(1)} %bitcast.61, pred[184]{0:T(512)(128)(4,1)S(1)} %iota_compare_fusion.2), kind=kOutput, calls=%fused_computation.11 | convolution fusion | flops 2316322048 | bytes 26215320 | tf_op jit(solution)/shard_map/rs,sif->rif/dot_general | solution.py:28
  223.3 2.1 copy.12
  225.4 0.0 reduce-scatter.5.cloned.1.call-update
  225.4 0.0 all-reduce.2.cloned.1.call-start
  225.5 0.0 reduce-scatter.3.cloned.1.call-done
  225.5 1.9 fusion.18
  227.4 0.0 all-reduce.2.cloned.1.call-update
  227.4 0.0 copy-done.2
  227.4 1.9 fusion.14
  229.3 70.3 %reduce-scatter.5.cloned.1.call-done = bf16[1024,128]{1,0:T(8,128)(2,1)} async-done(((bf16[8192,128]{1,0:T(8,128)(2,1)}), bf16[1024,128]{1,0:T(8,128)(2,1)}) %reduce-scatter.5.cloned.1.call-update) | async-done | bytes 262160 | tf_op jit(solution)/shard_map/reduce_scatter | solution.py:70
  299.6 0.0 copy-done.1
  299.6 1.7 fusion.16
  301.3 141.9 %all-reduce.2.cloned.1.call-done = f32[128,128]{1,0:T(8,128)} async-done(((f32[128,128]{1,0:T(8,128)}), f32[128,128]{1,0:T(8,128)}) %all-reduce.2.cloned.1.call-update) | async-done | bytes 65552 | tf_op jit(solution)/shard_map/psum | solution.py:63
  443.2 1.5 broadcast_multiply_fusion
  (4 shorter events, 0.0 us)
Async XLA Ops:
  7.2 2.0 copy-start
  7.2 60.7 %all-gather.6.cloned.1.call-start = ((), (), s32[]{:S(2)}) async-start(), calls=%async_computation.6 | async-start | bytes 2359296 | tf_op jit(solution)/shard_map/all_gather | solution.py:49
  9.1 140.1 %all-gather.4.cloned.1.call-start = ((), (), s32[]{:S(2)}) async-start(), calls=%async_computation.4 | async-start | bytes 4456448 | tf_op jit(solution)/shard_map/all_gather | solution.py:67
  10.9 214.6 %reduce-scatter.3.cloned.1.call-start = ((), (), s32[]{:S(2)}) async-start(), calls=%async_computation.2 | async-start | bytes 4456448 | tf_op jit(solution)/shard_map/reduce_scatter | solution.py:54
  99.1 24.6 %copy-start.3 = (s32[1,1,184]{2,1,0:T(1,128)S(1)}, s32[1,1,184]{2,1,0:T(1,128)}, u32[]{:S(2)}) copy-start(s32[1,1,184]{2,1,0:T(1,128)} %param.11) | copy-start | bytes 2212
  149.2 150.4 %reduce-scatter.5.cloned.1.call-start = ((), (), s32[]{:S(2)}) async-start(), calls=%async_computation.5 | async-start | bytes 2359296 | tf_op jit(solution)/shard_map/reduce_scatter | solution.py:70
  181.6 24.6 %copy-start.4 = (s32[1,1,184]{2,1,0:T(1,128)S(1)}, s32[1,1,184]{2,1,0:T(1,128)}, u32[]{:S(2)}) copy-start(s32[1,1,184]{2,1,0:T(1,128)} %param.12) | copy-start | bytes 2212
  206.2 21.2 %copy-start.2 = (bf16[128,128]{1,0:T(8,128)(2,1)S(1)}, bf16[128,128]{1,0:T(8,128)(2,1)}, u32[]{:S(2)}) copy-start(bf16[128,128]{1,0:T(8,128)(2,1)} %param.14) | copy-start | bytes 98308
  206.2 93.4 %copy-start.1 = (s32[1,1024,128]{2,1,0:T(8,128)S(1)}, s32[1,1024,128]{2,1,0:T(8,128)}, u32[]{:S(2)}) copy-start(s32[1,1024,128]{2,1,0:T(8,128)} %param.9) | copy-start | bytes 1572868
  225.4 217.8 %all-reduce.2.cloned.1.call-start = ((), (), s32[]{:S(2)}) async-start(), calls=%async_computation.3 | async-start | bytes 131072 | tf_op jit(solution)/shard_map/psum | solution.py:63
Sparse Core Ops, SparseCore 0:
  10.9 56.9 all-gather.5
  70.1 37.8 all-gather.3
  149.3 63.9 reduce-scatter.2
  225.6 74.0 reduce-scatter.4
  305.5 137.6 all-reduce.1
where the time goes:
time: 452 us; the launch traced here: 451 us
  waiting for transfers between devices  268 us (59%)
  matrix products  86.9 us (19%)
  local copies, waits for them, and re-layouts  75.9 us (17%)
  between operations  14.5 us (3%)
  other arithmetic  5.8 us (1%)
    psum x1, waiting for transfers between devices, body(): weight_grad = lax.psum(weight_term, ('row', 'col')) * grad_scale  142 us
    reduce_scatter x1, waiting for transfers between devices, body(): lax.psum_scatter(back_terms.astype(jnp.bfloat16), 'row', scatter_dimensio...  70.3 us
    all_gather x1, waiting for transfers between devices, body(): feat_panel = lax.all_gather(hidden, 'row', axis=0, tiled=True)  55.5 us
    dot_general x2, matrix products, apply_tiles(): jnp.einsum('rs,sif->rif', selector, products, precision=lax.Precision.HIG...  37.8 us
    dot_general x1, local copies, waits for them, and re-layouts, slot_products(): jnp.einsum('sij,sif->sjf', tile_vals, blocks, preferred_element_type=jnp....  24.6 us
    dot_general x1, local copies, waits for them, and re-layouts, slot_products(): jnp.einsum('sij,sjf->sif', tile_vals, blocks, preferred_element_type=jnp....  24.6 us
    dot_general x1, matrix products, slot_products(): jnp.einsum('sij,sif->sjf', tile_vals, blocks, preferred_element_type=jnp....  22 us
    dot_general x1, matrix products, slot_products(): jnp.einsum('sij,sjf->sif', tile_vals, blocks, preferred_element_type=jnp....  21.6 us
  transfers between devices with their start and end apart: 5, of which 3 were waited for; matrix products, arithmetic and copies ran while one was open for 37% of the time, Pallas kernels for 0%

commit v1 on v0

--- a/solution.py
+++ b/solution.py
@@ -60,7 +60,7 @@
         aggregate, cot_rows, (((0,), (0,)), ((), ())), preferred_element_type=jnp.float32
     )
     grad_scale = 1.0 / jnp.sqrt(jnp.float32(own_rows * lax.axis_size("row") * lax.axis_size("col")))
-    weight_grad = lax.psum(weight_term, ("row", "col")) * grad_scale
+    weight_grad = lax.psum(lax.psum(weight_term, "col"), "row") * grad_scale
     grad_rows = lax.dot_general(
         cot_rows, weight, (((1,), (1,)), ((), ())), preferred_element_type=jnp.float32
     )

time: 452 us -> 495 us (1.095)
  waiting for transfers between devices: 268 us -> 307 us
    psum x1 -> x2, waiting for transfers between devices: 142 us -> 166 us  [body(): weight_grad = lax.psum(lax.psum(weight_term, 'col'), 'row') * grad_scale]
    reduce_scatter x1, waiting for transfers between devices: 70.3 us -> 78.5 us  [body(): lax.psum_scatter(back_terms.astype(jnp.bfloat16), 'row', scatter_dimensio...]
    reduce_scatter x1, waiting for transfers between devices: 0.02 us -> 6.93 us  [body(): lax.psum_scatter(forward_terms.astype(jnp.bfloat16), 'col', scatter_dimen...]
  transfers between devices with their start and end apart: 5 -> 6, of which waited for: 3 -> 5; matrix products, arithmetic and copies ran while one was open for 37% -> 33% of each run, Pallas kernels for 0% -> 0%
where the time goes in v1:
time: 495 us; the launch traced here: 489 us
  waiting for transfers between devices  307 us (62%)
  matrix products  86 us (17%)
  local copies, waits for them, and re-layouts  75.9 us (15%)
  between operations  14.9 us (3%)
  other arithmetic  5.8 us (1%)
    psum x2, waiting for transfers between devices, body(): weight_grad = lax.psum(lax.psum(weight_term, 'col'), 'row') * grad_scale  166 us
    reduce_scatter x1, waiting for transfers between devices, body(): lax.psum_scatter(back_terms.astype(jnp.bfloat16), 'row', scatter_dimensio...  78.5 us
    all_gather x1, waiting for transfers between devices, body(): feat_panel = lax.all_gather(hidden, 'row', axis=0, tiled=True)  55.5 us
    dot_general x2, matrix products, apply_tiles(): jnp.einsum('rs,sif->rif', selector, products, precision=lax.Precision.HIG...  37.8 us
    dot_general x1, local copies, waits for them, and re-layouts, slot_products(): jnp.einsum('sij,sif->sjf', tile_vals, blocks, preferred_element_type=jnp....  24.7 us
    dot_general x1, local copies, waits for them, and re-layouts, slot_products(): jnp.einsum('sij,sjf->sif', tile_vals, blocks, preferred_element_type=jnp....  24.6 us
    dot_general x1, matrix products, slot_products(): jnp.einsum('sij,sif->sjf', tile_vals, blocks, preferred_element_type=jnp....  22.1 us
    dot_general x1, matrix products, slot_products(): jnp.einsum('sij,sjf->sif', tile_vals, blocks, preferred_element_type=jnp....  21.6 us
  transfers between devices with their start and end apart: 6, of which 5 were waited for; matrix products, arithmetic and copies ran while one was open for 33% of the time, Pallas kernels for 0%

profile of v1, /device:TPU:1, one launch (start us, length us, event | category | flops | bytes accessed | tf_op | source)
XLA Modules:
  0.0 489.5 jit_solution(13739604948537547541)
XLA Ops:
  7.2 0.0 copy-start
  7.2 0.0 all-gather.6.cloned.1.call-start
  7.2 1.9 convert_multiply_fusion
  9.1 0.0 all-gather.6.cloned.1.call-update
  9.1 0.0 all-gather.4.cloned.1.call-start
  9.2 0.0 copy-done
  9.2 1.7 convolution_convert_fusion
  10.9 0.0 all-gather.4.cloned.1.call-update
  10.9 0.0 reduce-scatter.3.cloned.1.call-start
  11.6 0.7 compare_select_fusion.1
  12.3 55.5 %all-gather.6.cloned.1.call-done = bf16[1,8192,128]{2,1,0:T(8,128)(2,1)} async-done(((bf16[1,1024,128]{2,1,0:T(8,128)(2,1)}), bf16[1,8192,128]{2,1,0:T(8,128)(2,1)}) %all-gather.6.cloned.1.call-update) | async-done | bytes 2097168 | tf_op jit(solution)/shard_map/all_gather | solution.py:49
  67.9 9.6 %gather_fusion = bf16[184,256,128]{2,1,0:T(8,128)(2,1)} fusion(bf16[32,256,128]{2,1,0:T(8,128)(2,1)} %bitcast.56, s32[1024]{0:T(1024)S(1)} %pad_clamp_fusion.1), kind=kCustom, calls=%fused_computation | custom fusion | bytes 24117984 | tf_op jit(solution)/shard_map/gather | solution.py:15
  77.5 21.6 %fusion.6 = f32[184,128,256]{2,1,0:T(8,128)} fusion(bf16[184,256,128]{2,1,0:T(8,128)(2,1)} %gather_fusion, bf16[1,1,184,256,256]{4,3,2,1,0:T(8,128)(2,1)} %param.10), kind=kOutput, calls=%fused_computation.8 | convolution fusion | flops 3087007744 | bytes 60293120 | tf_op jit(solution)/shard_map/sij,sjf->sif/dot_general | solution.py:16
  99.1 0.0 copy-start.4
  99.1 24.6 %copy.13 = f32[184,128,256]{1,0,2:T(8,128)} copy(f32[184,128,256]{2,1,0:T(8,128)} %fusion.6) | data formatting | bytes 48234496 | tf_op jit(solution)/shard_map/sij,sjf->sif/dot_general | solution.py:16
  123.7 0.0 copy-done.4
  123.7 20.8 %fusion.8 = bf16[64,256,128]{2,0,1:T(8,128)(2,1)S(1)} fusion(f32[184,128,256]{1,0,2:T(8,128)} %copy.13, s32[184]{0:T(256)S(1)} %bitcast.60, pred[184]{0:T(512)(128)(4,1)S(1)} %iota_compare_fusion.2), kind=kOutput, calls=%fused_computation.10 | convolution fusion | flops 4632644096 | bytes 28312472 | tf_op jit(solution)/shard_map/rs,sif->rif/dot_general | solution.py:28
  144.5 4.6 copy.11
  149.1 0.0 reduce-scatter.3.cloned.1.call-update
  149.2 0.0 all-reduce.3.cloned.1.call-start
  149.2 0.0 all-gather.4.cloned.1.call-done
  149.3 10.2 %gather_fusion.1 = bf16[184,256,128]{2,1,0:T(8,128)(2,1)} fusion(bf16[64,256,128]{2,1,0:T(8,128)(2,1)} %bitcast.57, s32[1024]{0:T(1024)S(1)} %pad_clamp_fusion), kind=kCustom, calls=%fused_computation.1 | custom fusion | bytes 24117984 | tf_op jit(solution)/shard_map/gather | solution.py:11
  159.5 22.1 %fusion.4 = f32[184,128,256]{2,1,0:T(8,128)} fusion(bf16[184,256,128]{2,1,0:T(8,128)(2,1)} %gather_fusion.1, bf16[1,1,184,256,256]{4,3,2,1,0:T(8,128)(2,1)} %param.10), kind=kOutput, calls=%fused_computation.6 | convolution fusion | flops 3087007744 | bytes 60293120 | tf_op jit(solution)/shard_map/sij,sif->sjf/dot_general | solution.py:12
  181.6 0.0 copy-start.5
  181.6 24.7 %copy.14 = f32[184,128,256]{1,0,2:T(8,128)} copy(f32[184,128,256]{2,1,0:T(8,128)} %fusion.4) | data formatting | bytes 48234496 | tf_op jit(solution)/shard_map/sij,sif->sjf/dot_general | solution.py:12
  206.3 6.9 %reduce-scatter.3.cloned.1.call-done = bf16[1024,128]{1,0:T(8,128)(2,1)} async-done(((bf16[16384,128]{1,0:T(8,128)(2,1)}), bf16[1024,128]{1,0:T(8,128)(2,1)}) %reduce-scatter.3.cloned.1.call-update) | async-done | bytes 262160 | tf_op jit(solution)/shard_map/reduce_scatter | solution.py:54
  213.2 1.8 fusion.18
  215.1 0.0 all-reduce.3.cloned.1.call-update
  215.1 0.0 reduce-scatter.5.cloned.1.call-start
  215.1 0.0 copy-done.5
  215.1 0.0 copy-start.2
  215.2 0.0 copy-start.3
  215.2 0.0 copy-start.1
  215.2 17.1 %fusion.11 = bf16[32,256,128]{2,0,1:T(8,128)(2,1)S(1)} fusion(f32[184,128,256]{1,0,2:T(8,128)} %copy.14, s32[184]{0:T(256)S(1)} %bitcast.61, pred[184]{0:T(512)(128)(4,1)S(1)} %iota_compare_fusion.2), kind=kOutput, calls=%fused_computation.11 | convolution fusion | flops 2316322048 | bytes 26215320 | tf_op jit(solution)/shard_map/rs,sif->rif/dot_general | solution.py:28
  232.2 2.1 copy.12
  234.4 0.0 reduce-scatter.5.cloned.1.call-update
  234.4 0.0 all-reduce.5.cloned.1.call-start
  234.5 0.0 copy-done.2
  234.5 0.0 copy-done.3
  234.5 0.9 fusion.14
  235.4 87.0 %all-reduce.3.cloned.1.call-done = f32[128,128]{1,0:T(8,128)} async-done(((f32[128,128]{1,0:T(8,128)}), f32[128,128]{1,0:T(8,128)}) %all-reduce.3.cloned.1.call-update) | async-done | bytes 65552 | tf_op jit(solution)/shard_map/psum | solution.py:63
  322.4 0.0 all-reduce.5.cloned.1.call-update
  322.4 78.5 %reduce-scatter.5.cloned.1.call-done = bf16[1024,128]{1,0:T(8,128)(2,1)} async-done(((bf16[8192,128]{1,0:T(8,128)(2,1)}), bf16[1024,128]{1,0:T(8,128)(2,1)}) %reduce-scatter.5.cloned.1.call-update) | async-done | bytes 262160 | tf_op jit(solution)/shard_map/reduce_scatter | solution.py:70
  400.9 0.0 copy-done.1
  400.9 1.7 fusion.16
  402.6 78.5 %all-reduce.5.cloned.1.call-done = f32[128,128]{1,0:T(8,128)} async-done(((f32[128,128]{1,0:T(8,128)}), f32[128,128]{1,0:T(8,128)}) %all-reduce.5.cloned.1.call-update) | async-done | bytes 65552 | tf_op jit(solution)/shard_map/psum | solution.py:63
  481.2 1.5 broadcast_multiply_fusion
  (4 shorter events, 0.0 us)
Async XLA Ops:
  7.2 2.0 copy-start
  7.2 60.7 %all-gather.6.cloned.1.call-start = ((), (), s32[]{:S(2)}) async-start(), calls=%async_computation.7 | async-start | bytes 2359296 | tf_op jit(solution)/shard_map/all_gather | solution.py:49
  9.1 140.1 %all-gather.4.cloned.1.call-start = ((), (), s32[]{:S(2)}) async-start(), calls=%async_computation.5 | async-start | bytes 4456448 | tf_op jit(solution)/shard_map/all_gather | solution.py:67
  10.9 202.3 %reduce-scatter.3.cloned.1.call-start = ((), (), s32[]{:S(2)}) async-start(), calls=%async_computation.2 | async-start | bytes 4456448 | tf_op jit(solution)/shard_map/reduce_scatter | solution.py:54
  99.1 24.6 %copy-start.4 = (s32[1,1,184]{2,1,0:T(1,128)S(1)}, s32[1,1,184]{2,1,0:T(1,128)}, u32[]{:S(2)}) copy-start(s32[1,1,184]{2,1,0:T(1,128)} %param.11) | copy-start | bytes 2212
  149.2 173.2 %all-reduce.3.cloned.1.call-start = ((), (), s32[]{:S(2)}) async-start(), calls=%async_computation.3 | async-start | bytes 131072 | tf_op jit(solution)/shard_map/psum | solution.py:63
  181.6 33.5 %copy-start.5 = (s32[1,1,184]{2,1,0:T(1,128)S(1)}, s32[1,1,184]{2,1,0:T(1,128)}, u32[]{:S(2)}) copy-start(s32[1,1,184]{2,1,0:T(1,128)} %param.12) | copy-start | bytes 2212
  215.1 185.8 %reduce-scatter.5.cloned.1.call-start = ((), (), s32[]{:S(2)}) async-start(), calls=%async_computation.6 | async-start | bytes 2359296 | tf_op jit(solution)/shard_map/reduce_scatter | solution.py:70
  215.1 19.3 %copy-start.2 = (bf16[1024,128]{1,0:T(8,128)(2,1)S(1)}, bf16[1024,128]{1,0:T(8,128)(2,1)}, u32[]{:S(2)}) copy-start(bf16[1024,128]{1,0:T(8,128)(2,1)} %reduce-scatter.3.cloned.1.call-done) | copy-start | bytes 786436
  215.2 19.3 %copy-start.3 = (bf16[128,128]{1,0:T(8,128)(2,1)S(1)}, bf16[128,128]{1,0:T(8,128)(2,1)}, u32[]{:S(2)}) copy-start(bf16[128,128]{1,0:T(8,128)(2,1)} %param.14) | copy-start | bytes 98308
  215.2 185.7 %copy-start.1 = (s32[1,1024,128]{2,1,0:T(8,128)S(1)}, s32[1,1024,128]{2,1,0:T(8,128)}, u32[]{:S(2)}) copy-start(s32[1,1024,128]{2,1,0:T(8,128)} %param.9) | copy-start | bytes 1572868
  234.4 246.8 %all-reduce.5.cloned.1.call-start = ((), (), s32[]{:S(2)}) async-start(), calls=%async_computation.4 | async-start | bytes 131072 | tf_op jit(solution)/shard_map/psum | solution.py:63
Sparse Core Ops, SparseCore 0:
  10.9 56.9 all-gather.5
  70.1 37.8 all-gather.3
  149.3 63.8 reduce-scatter.2
  216.1 106.2 all-reduce.2
  326.5 74.3 reduce-scatter.4
  403.2 77.9 all-reduce.4
